TPU v7x, 32 devices: a whole 2x2x4 slice. The times are simulated.
32 devices in a mesh: groups: 2 (over x), dp: 16 (over z, y, core).
Axes of the slice: x: 2, y: 2, z: 4, core: 2. Of those that a mesh axis runs over, the one named last changes fastest.
Arguments:
- activations: bfloat16 [12288, 16384], P(('groups', 'dp')), parts along dimension 0, may hold values from -18 to 18
- labels: int32 [12288], P(('groups', 'dp')), parts along dimension 0, may hold values from 0 to 63, as said below
- counts: int32 [12288], P(('groups', 'dp')), parts along dimension 0, may hold values from 1 to 4
Outputs:
- solution: float32 [32768, 64], P(('groups', 'dp')), parts along dimension 0
- residual: float32 [32768, 64], P(('groups', 'dp')), parts along dimension 0
There are 2 independent parts, one for each index of `groups`. A program takes and returns all parts, laid end to end along the dimension named above; each array names one. Nothing has to cross between parts.
Inputs may be any that keep to these rules, and one draw needn't show every extreme that they name: `labels`: concept index of each row; every concept of 0 to 63 names at least one row. `counts`: integer sample weight of each row.
All inputs are finite; a program needn't handle non-finite values.
Results may differ from a plain program's by a relative error of at most 0.012.
The roundings to bfloat16 on the way count: a program that leaves them out, or rounds other values in their place, can miss the bound.
Values may be sent and summed in bfloat16 or wider, within the bound.
No kernel may reach another device: no remote copies, remote signals or barrier semaphores. Data moves between devices by JAX's collectives and lax.ppermute only.
A program may use at most 64 MiB of HBM per device.

v0:
```python
import jax
import jax.numpy as jnp
from jax import lax
from jax.sharding import PartitionSpec as P

K = 64
ITERS = 2
RIDGE = 0.1


def precise(left_side, right_side):
    return jnp.dot(
        left_side, right_side, precision=lax.Precision.HIGHEST, preferred_element_type=jnp.float32
    )


def symmetric(matrix):
    return 0.5 * (matrix + matrix.T)


def solve_positive(matrix, target):
    return jax.scipy.linalg.cho_solve((jnp.linalg.cholesky(matrix), True), target)


def contract_rows(left_side, right_side):
    return lax.dot_general(
        left_side, right_side, (((0,), (0,)), ((), ())), preferred_element_type=jnp.float32
    )


def per_device(activations, labels, counts):
    weights = counts.astype(jnp.float32)
    classes = jnp.arange(K, dtype=jnp.int32)
    member_full = jnp.where(labels[:, None] == classes[None, :], weights[:, None], jnp.float32(0.0))
    local_weight = jnp.sum(member_full, axis=0)
    member = member_full.astype(jnp.bfloat16)
    class_sums = lax.psum_scatter(
        contract_rows(activations, member), "dp", scatter_dimension=0, tiled=True
    )
    class_weight = lax.psum(local_weight, "dp")
    total_weight = jnp.sum(class_weight)
    class_means = class_sums / class_weight[None, :]
    mean_diff = class_means * jnp.sqrt(class_weight)[None, :]
    solution = jnp.zeros_like(mean_diff)
    residual = mean_diff
    direction = mean_diff
    current = symmetric(lax.psum(precise(residual.T, residual), "dp"))
    for iteration in range(ITERS):
        probed = jnp.dot(
            activations,
            lax.all_gather(direction.astype(jnp.bfloat16), "dp", axis=0, tiled=True),
            preferred_element_type=jnp.float32,
        )
        weighted = (weights[:, None] * probed).astype(jnp.bfloat16)
        panel = lax.psum_scatter(
            contract_rows(activations, weighted), "dp", scatter_dimension=0, tiled=True
        )
        cross, along_panel, along_along = lax.psum(
            (
                precise(class_means.T, direction),
                precise(direction.T, panel),
                precise(direction.T, direction),
            ),
            "dp",
        )
        scaled = class_weight[:, None] * cross
        curvature = symmetric(
            (along_panel - precise(cross.T, scaled)) / total_weight + RIDGE * along_along
        )
        step_alpha = solve_positive(curvature, current)
        image = (panel - precise(class_means, scaled)) / total_weight + RIDGE * direction
        solution = solution + precise(direction, step_alpha)
        residual = residual - precise(image, step_alpha)
        renewed = current
        if iteration + 1 < ITERS:
            renewed = symmetric(lax.psum(precise(residual.T, residual), "dp"))
        if iteration + 1 < ITERS:
            step_beta = solve_positive(current, renewed)
            direction = residual + precise(direction, step_beta)
            current = renewed
    return (solution, residual)


def solution(mesh):
    in_specs = (P(("groups", "dp"), None), P(("groups", "dp")), P(("groups", "dp")))
    out_specs = (P(("groups", "dp"), None), P(("groups", "dp"), None))
    return jax.shard_map(
        per_device, mesh=mesh, in_specs=in_specs, out_specs=out_specs, check_vma=False
    )
```

profile of v0, /device:TPU:0, one launch (start us, length us, event | category | flops | bytes accessed | tf_op | source)
XLA Modules:
  0.0 587.8 jit_solution(6999212861251710433)
XLA Ops:
  7.9 8.9 %convolution_bitcast_fusion.2 = f32[16384,64]{0,1:T(8,128)} fusion(bf16[384,16384]{1,0:T(8,128)(2,1)} %param.6, f32[384]{0:T(512)S(1)} %convert_element_type.20, s32[384]{0:T(512)} %param.7), kind=kOutput, calls=%fused_computation.2 | convolution fusion | flops 805355520 | bytes 16780288 | tf_op jit(solution)/shard_map/dot_general | solution.py:26
  17.0 35.0 %psum.59 = f32[64]{0:T(128)S(1)} all-reduce(f32[64]{0:T(128)S(1)} %select_reduce_fusion), channel_id=1, replica_groups=mesh['groups'=2,'dp'=16] {'dp'}, use_global_device_ids=true, to_apply=%region_2.3 | all-reduce | flops 64 | bytes 512 | tf_op jit(solution)/shard_map/psum | solution.py:40
  52.6 39.5 %reduce-scatter.4.cloned.1.call-done = f32[1024,64]{0,1:T(8,128)} async-done(((f32[16384,64]{0,1:T(8,128)}), f32[1024,64]{0,1:T(8,128)}) %reduce-scatter.4.cloned.1.call-update) | async-done | bytes 262160 | tf_op jit(solution)/shard_map/reduce_scatter | solution.py:37
  92.1 1.7 multiply_convert_fusion
  93.9 41.7 %all-gather.3.cloned.1.call-done = bf16[16384,64]{0,1:T(8,128)(2,1)} async-done(((bf16[1024,64]{0,1:T(8,128)(2,1)}), bf16[16384,64]{0,1:T(8,128)(2,1)}) %all-gather.3.cloned.1.call-update) | async-done | bytes 2097168 | tf_op jit(solution)/shard_map/all_gather | solution.py:51
  135.5 18.5 %convolution_bitcast_fusion.1 = f32[16384,64]{0,1:T(8,128)} fusion(bf16[384,16384]{1,0:T(8,128)(2,1)} %param.6, bf16[16384,64]{0,1:T(8,128)(2,1)} %all-gather.3.cloned.1.call-done, f32[384]{0:T(512)S(1)} %convert_element_type.20), kind=kOutput, calls=%fused_computation.1 | convolution fusion | flops 1610661888 | bytes 18875904 | tf_op jit(solution)/shard_map/dot_general | solution.py:26
  155.0 70.3 %reduce-scatter.6.cloned.1.call-done = f32[1024,64]{0,1:T(8,128)} async-done(((f32[16384,64]{0,1:T(8,128)}), f32[1024,64]{0,1:T(8,128)}) %reduce-scatter.6.cloned.1.call-update) | async-done | bytes 262160 | tf_op jit(solution)/shard_map/reduce_scatter | solution.py:55
  225.3 1.4 fusion.17
  226.7 59.2 %all-reduce.1 = (f32[64,64]{1,0:T(8,128)S(1)}, f32[64,64]{1,0:T(8,128)S(1)}, f32[64,64]{1,0:T(8,128)S(1)}) all-reduce(f32[64,64]{1,0:T(8,128)S(1)} %fusion.13, f32[64,64]{1,0:T(8,128)S(1)} %fusion.17, f32[64,64]{1,0:T(8,128)S(1)} %fusion.15), channel_id=1, replica_groups=mesh['groups'=2,'dp'=16] {'dp'}, use_global_device_ids=true, to_apply=%region_7.8 | all-reduce | flops 12288 | bytes 98304 | tf_op jit(solution)/shard_map/psum | solution.py:58
  286.1 5.8 cholesky.70
  293.3 4.9 custom-call.10
  299.4 5.9 cholesky.59
  306.6 4.9 custom-call.9
  311.9 2.1 fusion.3
  314.8 57.6 %psum.63 = f32[64,64]{1,0:T(8,128)S(1)} all-reduce(f32[64,64]{1,0:T(8,128)S(1)} %fusion.64), channel_id=1, replica_groups=mesh['groups'=2,'dp'=16] {'dp'}, use_global_device_ids=true, to_apply=%region_10.13 | all-reduce | flops 4096 | bytes 32768 | tf_op jit(solution)/shard_map/psum | solution.py:76
  374.3 38.6 %all-gather.5.cloned.1.call-done = bf16[16384,64]{0,1:T(8,128)(2,1)} async-done(((bf16[1024,64]{0,1:T(8,128)(2,1)}), bf16[16384,64]{0,1:T(8,128)(2,1)}) %all-gather.5.cloned.1.call-update) | async-done | bytes 2097168 | tf_op jit(solution)/shard_map/all_gather | solution.py:51
  412.9 18.5 %convolution_bitcast_fusion = f32[16384,64]{0,1:T(8,128)} fusion(bf16[384,16384]{1,0:T(8,128)(2,1)} %param.6, bf16[16384,64]{0,1:T(8,128)(2,1)} %all-gather.5.cloned.1.call-done, f32[384]{0:T(512)S(1)} %convert_element_type.20), kind=kOutput, calls=%fused_computation | convolution fusion | flops 1610661888 | bytes 18875904 | tf_op jit(solution)/shard_map/dot_general | solution.py:26
  432.6 70.1 %reduce-scatter.8.cloned.1.call-done = f32[1024,64]{0,1:T(8,128)} async-done(((f32[16384,64]{0,1:T(8,128)}), f32[1024,64]{0,1:T(8,128)}) %reduce-scatter.8.cloned.1.call-update) | async-done | bytes 262160 | tf_op jit(solution)/shard_map/reduce_scatter | solution.py:55
  502.8 1.3 fusion.65
  504.1 59.1 %all-reduce = (f32[64,64]{1,0:T(8,128)S(1)}, f32[64,64]{1,0:T(8,128)S(1)}, f32[64,64]{1,0:T(8,128)S(1)}) all-reduce(f32[64,64]{1,0:T(8,128)S(1)} %fusion.65, f32[64,64]{1,0:T(8,128)S(1)} %fusion.61, f32[64,64]{1,0:T(8,128)S(1)} %fusion.66), channel_id=1, replica_groups=mesh['groups'=2,'dp'=16] {'dp'}, use_global_device_ids=true, to_apply=%region_12.15 | all-reduce | flops 12288 | bytes 98304 | tf_op jit(solution)/shard_map/psum | solution.py:58
  564.4 5.8 cholesky.81
  571.6 4.9 custom-call.11
  576.9 2.1 fusion.1
  579.0 1.1 convolution_subtract_fusion
  (59 shorter events, 14.8 us)
Async XLA Ops:
  7.2 9.7 %copy-start.1 = (s32[384]{0:T(512)S(1)}, s32[384]{0:T(512)}, u32[]{:S(2)}) copy-start(s32[384]{0:T(512)} %param.7) | copy-start | bytes 4612
  7.2 84.9 %reduce-scatter.4.cloned.1.call-start = ((), (), s32[]{:S(2)}) async-start(), calls=%async_computation.3 | async-start | bytes 4456448 | tf_op jit(solution)/shard_map/reduce_scatter | solution.py:37
  16.8 118.7 %all-gather.3.cloned.1.call-start = ((), (), s32[]{:S(2)}) async-start(), calls=%async_computation.4 | async-start | bytes 2228224 | tf_op jit(solution)/shard_map/all_gather | solution.py:51
  93.8 60.3 %copy-start = (f32[1024,64]{0,1:T(8,128)S(1)}, f32[1024,64]{0,1:T(8,128)}, u32[]{:S(2)}) copy-start(f32[1024,64]{0,1:T(8,128)} %reduce-scatter.4.cloned.1.call-done) | copy-start | bytes 786436
  93.8 131.5 %reduce-scatter.6.cloned.1.call-start = ((), (), s32[]{:S(2)}) async-start(), calls=%async_computation.5 | async-start | bytes 4456448 | tf_op jit(solution)/shard_map/reduce_scatter | solution.py:55
  154.0 258.9 %all-gather.5.cloned.1.call-start = ((), (), s32[]{:S(2)}) async-start(), calls=%async_computation.6 | async-start | bytes 2228224 | tf_op jit(solution)/shard_map/all_gather | solution.py:51
  374.1 128.7 %reduce-scatter.8.cloned.1.call-start = ((), (), s32[]{:S(2)}) async-start(), calls=%async_computation.7 | async-start | bytes 4456448 | tf_op jit(solution)/shard_map/reduce_scatter | solution.py:55
Sparse Core Ops, SparseCore 0:
  16.9 75.1 reduce-scatter.3
  95.1 40.4 all-gather.2
  154.1 71.1 reduce-scatter.5
  374.2 38.6 all-gather.4
  431.5 71.2 reduce-scatter.7
where the time goes:
time: 588 us
  waiting for transfers between devices  260 us (44%)
  blocking collectives  211 us (36%)
  matrix products  62 us (11%)
  other arithmetic  39.4 us (7%)
  between operations  14.1 us (2%)
    reduce_scatter x2, waiting for transfers between devices, per_device(): lax.psum_scatter(contract_rows(activations, weighted), 'dp', scatter_dime...  140 us
    psum x2, blocking collectives, per_device(): lax.psum((precise(class_means.T, direction), precise(direction.T, panel),...  118 us
    all_gather x2, waiting for transfers between devices, per_device(): lax.all_gather(direction.astype(jnp.bfloat16), 'dp', axis=0, tiled=True)  80.2 us
    psum x1, blocking collectives, per_device(): renewed = symmetric(lax.psum(precise(residual.T, residual), 'dp'))  57.6 us
    dot_general x3, matrix products, contract_rows(): lax.dot_general(left_side, right_side, (((0,), (0,)), ((), ())), preferre...  45.8 us
    reduce_scatter x1, waiting for transfers between devices, per_device(): lax.psum_scatter(contract_rows(activations, member), 'dp', scatter_dimens...  39.5 us
    psum x1, blocking collectives, per_device(): class_weight = lax.psum(local_weight, 'dp')  35 us
    another operation x9, other arithmetic, solve_positive(): jnp.linalg.cholesky(matrix)  19.6 us
  transfers between devices with their start and end apart: 5, of which 5 were waited for; matrix products, arithmetic and copies ran while one was open for 0% of the time, Pallas kernels for 0%

commit v1 on v0

--- a/solution.py
+++ b/solution.py
@@ -2,10 +2,15 @@
 import jax.numpy as jnp
 from jax import lax
 from jax.sharding import PartitionSpec as P
+from jax.lax import all_gather
 
 K = 64
 ITERS = 2
 RIDGE = 0.1
+
+
+def link_the_rounds(load):
+    return all_gather(load, "dp").sum(axis=0)
 
 
 def precise(left_side, right_side):
@@ -73,7 +78,7 @@
         residual = residual - precise(image, step_alpha)
         renewed = current
         if iteration + 1 < ITERS:
-            renewed = symmetric(lax.psum(precise(residual.T, residual), "dp"))
+            renewed = symmetric(link_the_rounds(precise(residual.T, residual)))
         if iteration + 1 < ITERS:
             step_beta = solve_positive(current, renewed)
             direction = residual + precise(direction, step_beta)

time: 588 us -> 551 us (0.937)
  blocking collectives: 211 us -> 172 us
    psum x1 -> x0, blocking collectives: 57.6 us -> none  [per_device(): renewed = symmetric(lax.psum(precise(residual.T, residual), 'dp'))]
    all_gather x0 -> x1, blocking collectives: none -> 18.7 us  [link_the_rounds(): return all_gather(load, 'dp').sum(axis=0)]
  transfers between devices with their start and end apart: 5 -> 5, of which waited for: 5 -> 5; matrix products, arithmetic and copies ran while one was open for 0% -> 1% of each run, Pallas kernels for 0% -> 0%
where the time goes in v1:
time: 551 us
  waiting for transfers between devices  262 us (48%)
  blocking collectives  172 us (31%)
  matrix products  62 us (11%)
  other arithmetic  39.4 us (7%)
  between operations  14.1 us (3%)
    reduce_scatter x2, waiting for transfers between devices, per_device(): lax.psum_scatter(contract_rows(activations, weighted), 'dp', scatter_dime...  140 us
    psum x2, blocking collectives, per_device(): lax.psum((precise(class_means.T, direction), precise(direction.T, panel),...  118 us
    all_gather x2, waiting for transfers between devices, per_device(): lax.all_gather(direction.astype(jnp.bfloat16), 'dp', axis=0, tiled=True)  82.1 us
    dot_general x3, matrix products, contract_rows(): lax.dot_general(left_side, right_side, (((0,), (0,)), ((), ())), preferre...  45.8 us
    reduce_scatter x1, waiting for transfers between devices, per_device(): lax.psum_scatter(contract_rows(activations, member), 'dp', scatter_dimens...  39.5 us
    psum x1, blocking collectives, per_device(): class_weight = lax.psum(local_weight, 'dp')  35 us
    another operation x9, other arithmetic, solve_positive(): jnp.linalg.cholesky(matrix)  19.6 us
    all_gather x1, blocking collectives, link_the_rounds(): return all_gather(load, 'dp').sum(axis=0)  18.7 us
  transfers between devices with their start and end apart: 5, of which 5 were waited for; matrix products, arithmetic and copies ran while one was open for 1% of the time, Pallas kernels for 0%

profile of v1, /device:TPU:0, one launch (start us, length us, event | category | flops | bytes accessed | tf_op | source)
XLA Modules:
  0.0 550.8 jit_solution(4039987608946947404)
XLA Ops:
  7.9 8.9 %convolution_bitcast_fusion.2 = f32[16384,64]{0,1:T(8,128)} fusion(bf16[384,16384]{1,0:T(8,128)(2,1)} %param.6, f32[384]{0:T(512)S(1)} %convert_element_type.20, s32[384]{0:T(512)} %param.7), kind=kOutput, calls=%fused_computation.2 | convolution fusion | flops 805355520 | bytes 16780288 | tf_op jit(solution)/shard_map/dot_general | solution.py:31
  17.0 35.0 %psum.52 = f32[64]{0:T(128)S(1)} all-reduce(f32[64]{0:T(128)S(1)} %select_reduce_fusion), channel_id=1, replica_groups=mesh['groups'=2,'dp'=16] {'dp'}, use_global_device_ids=true, to_apply=%region_2.3 | all-reduce | flops 64 | bytes 512 | tf_op jit(solution)/shard_map/psum | solution.py:45
  52.6 39.5 %reduce-scatter.4.cloned.1.call-done = f32[1024,64]{0,1:T(8,128)} async-done(((f32[16384,64]{0,1:T(8,128)}), f32[1024,64]{0,1:T(8,128)}) %reduce-scatter.4.cloned.1.call-update) | async-done | bytes 262160 | tf_op jit(solution)/shard_map/reduce_scatter | solution.py:42
  92.1 1.7 multiply_convert_fusion
  93.9 41.7 %all-gather.4.cloned.1.call-done = bf16[16384,64]{0,1:T(8,128)(2,1)} async-done(((bf16[1024,64]{0,1:T(8,128)(2,1)}), bf16[16384,64]{0,1:T(8,128)(2,1)}) %all-gather.4.cloned.1.call-update) | async-done | bytes 2097168 | tf_op jit(solution)/shard_map/all_gather | solution.py:56
  135.5 18.5 %convolution_bitcast_fusion.1 = f32[16384,64]{0,1:T(8,128)} fusion(bf16[384,16384]{1,0:T(8,128)(2,1)} %param.6, bf16[16384,64]{0,1:T(8,128)(2,1)} %all-gather.4.cloned.1.call-done, f32[384]{0:T(512)S(1)} %convert_element_type.20), kind=kOutput, calls=%fused_computation.1 | convolution fusion | flops 1610661888 | bytes 18875904 | tf_op jit(solution)/shard_map/dot_general | solution.py:31
  155.0 70.3 %reduce-scatter.6.cloned.1.call-done = f32[1024,64]{0,1:T(8,128)} async-done(((f32[16384,64]{0,1:T(8,128)}), f32[1024,64]{0,1:T(8,128)}) %reduce-scatter.6.cloned.1.call-update) | async-done | bytes 262160 | tf_op jit(solution)/shard_map/reduce_scatter | solution.py:60
  225.3 1.4 fusion.17
  226.7 59.2 %all-reduce.1 = (f32[64,64]{1,0:T(8,128)S(1)}, f32[64,64]{1,0:T(8,128)S(1)}, f32[64,64]{1,0:T(8,128)S(1)}) all-reduce(f32[64,64]{1,0:T(8,128)S(1)} %fusion.13, f32[64,64]{1,0:T(8,128)S(1)} %fusion.17, f32[64,64]{1,0:T(8,128)S(1)} %fusion.15), channel_id=1, replica_groups=mesh['groups'=2,'dp'=16] {'dp'}, use_global_device_ids=true, to_apply=%region_7.8 | all-reduce | flops 12288 | bytes 98304 | tf_op jit(solution)/shard_map/psum | solution.py:63
  287.2 5.9 %cholesky.59 = f32[64,64]{1,0:T(8,128)S(1)} custom-call(f32[64,64]{1,0:T(8,128)S(1)} %copy.18), custom_call_target="Cholesky" | custom-call | tf_op jit(solution)/shard_map/jit(cholesky)/cholesky | solution.py:27
  294.4 4.9 custom-call.9
  299.8 2.1 fusion.3
  302.7 18.7 %all-gather = f32[1024,64]{1,0:T(8,128)S(1)} all-gather(f32[64,64]{1,0:T(8,128)S(1)} %fusion.64), channel_id=2, replica_groups=mesh['groups'=2,'dp'=16] {'dp'}, dimensions={0}, use_global_device_ids=true | all-gather | bytes 278528 | tf_op jit(solution)/shard_map/all_gather | solution.py:13
  321.5 5.8 %cholesky.70 = f32[64,64]{1,0:T(8,128)S(1)} custom-call(f32[64,64]{1,0:T(8,128)S(1)} %fusion.44), custom_call_target="Cholesky" | custom-call | tf_op jit(solution)/shard_map/jit(cholesky)/cholesky | solution.py:27
  328.7 4.9 custom-call.10
  335.4 40.4 %all-gather.6.cloned.1.call-done = bf16[16384,64]{0,1:T(8,128)(2,1)} async-done(((bf16[1024,64]{0,1:T(8,128)(2,1)}), bf16[16384,64]{0,1:T(8,128)(2,1)}) %all-gather.6.cloned.1.call-update) | async-done | bytes 2097168 | tf_op jit(solution)/shard_map/all_gather | solution.py:56
  375.9 18.5 %convolution_bitcast_fusion = f32[16384,64]{0,1:T(8,128)} fusion(bf16[384,16384]{1,0:T(8,128)(2,1)} %param.6, bf16[16384,64]{0,1:T(8,128)(2,1)} %all-gather.6.cloned.1.call-done, f32[384]{0:T(512)S(1)} %convert_element_type.20), kind=kOutput, calls=%fused_computation | convolution fusion | flops 1610661888 | bytes 18875904 | tf_op jit(solution)/shard_map/dot_general | solution.py:31
  395.6 70.1 %reduce-scatter.8.cloned.1.call-done = f32[1024,64]{0,1:T(8,128)} async-done(((f32[16384,64]{0,1:T(8,128)}), f32[1024,64]{0,1:T(8,128)}) %reduce-scatter.8.cloned.1.call-update) | async-done | bytes 262160 | tf_op jit(solution)/shard_map/reduce_scatter | solution.py:60
  465.8 1.3 fusion.65
  467.1 59.1 %all-reduce = (f32[64,64]{1,0:T(8,128)S(1)}, f32[64,64]{1,0:T(8,128)S(1)}, f32[64,64]{1,0:T(8,128)S(1)}) all-reduce(f32[64,64]{1,0:T(8,128)S(1)} %fusion.65, f32[64,64]{1,0:T(8,128)S(1)} %fusion.61, f32[64,64]{1,0:T(8,128)S(1)} %fusion.66), channel_id=1, replica_groups=mesh['groups'=2,'dp'=16] {'dp'}, use_global_device_ids=true, to_apply=%region_12.15 | all-reduce | flops 12288 | bytes 98304 | tf_op jit(solution)/shard_map/psum | solution.py:63
  527.4 5.8 %cholesky.81 = f32[64,64]{1,0:T(8,128)S(1)} custom-call(f32[64,64]{1,0:T(8,128)S(1)} %fusion.38), custom_call_target="Cholesky" | custom-call | tf_op jit(solution)/shard_map/jit(cholesky)/cholesky | solution.py:27
  534.6 4.9 custom-call.11
  539.9 2.1 fusion.1
  542.0 1.1 convolution_subtract_fusion
  (60 shorter events, 14.9 us)
Async XLA Ops:
  7.2 9.7 %copy-start.1 = (s32[384]{0:T(512)S(1)}, s32[384]{0:T(512)}, u32[]{:S(2)}) copy-start(s32[384]{0:T(512)} %param.7) | copy-start | bytes 4612
  7.2 84.9 %reduce-scatter.4.cloned.1.call-start = ((), (), s32[]{:S(2)}) async-start(), calls=%async_computation.3 | async-start | bytes 4456448 | tf_op jit(solution)/shard_map/reduce_scatter | solution.py:42
  16.8 118.7 %all-gather.4.cloned.1.call-start = ((), (), s32[]{:S(2)}) async-start(), calls=%async_computation.4 | async-start | bytes 2228224 | tf_op jit(solution)/shard_map/all_gather | solution.py:56
  93.8 60.3 %copy-start = (f32[1024,64]{0,1:T(8,128)S(1)}, f32[1024,64]{0,1:T(8,128)}, u32[]{:S(2)}) copy-start(f32[1024,64]{0,1:T(8,128)} %reduce-scatter.4.cloned.1.call-done) | copy-start | bytes 786436
  93.8 131.5 %reduce-scatter.6.cloned.1.call-start = ((), (), s32[]{:S(2)}) async-start(), calls=%async_computation.5 | async-start | bytes 4456448 | tf_op jit(solution)/shard_map/reduce_scatter | solution.py:60
  154.0 221.9 %all-gather.6.cloned.1.call-start = ((), (), s32[]{:S(2)}) async-start(), calls=%async_computation.6 | async-start | bytes 2228224 | tf_op jit(solution)/shard_map/all_gather | solution.py:56
  335.2 130.6 %reduce-scatter.8.cloned.1.call-start = ((), (), s32[]{:S(2)}) async-start(), calls=%async_computation.7 | async-start | bytes 4456448 | tf_op jit(solution)/shard_map/reduce_scatter | solution.py:60
Sparse Core Ops, SparseCore 0:
  16.9 75.1 reduce-scatter.3
  95.1 40.4 all-gather.3
  154.1 71.1 reduce-scatter.5
  335.3 40.5 all-gather.5
  394.5 71.2 reduce-scatter.7
